TPU v7x, 256 devices: a whole 4x4x8 slice. The times are simulated.
256 devices in a mesh: hb: 4 (over y), row: 16 (over z, x_hi), col: 4 (over x_lo, core).
Axes of the slice: x: 4 (x_hi: 2, x_lo: 2; x = x_hi * 2 + x_lo), y: 4, z: 8, core: 2. Of those that a mesh axis runs over, the one named last changes fastest.
Arguments:
- cell_state: float32 [256, 8, 256, 512], P('hb', None, 'row', 'col'), may hold values from -6 to 6
- normalizer: float32 [256, 8, 256], P('hb', None, 'row'), may hold values from 0.1 to 4
- stabilizer: float32 [256, 8, 16], P('hb', None, 'row'), may hold values from -5 to 120
- queries: float32 [256, 8, 256], P('hb', None, 'row'), may hold values from 0.0125 to 0.1125
- key_vectors: float32 [256, 8, 256], P('hb', None, 'row'), may hold values from -6 to 6
- token_value_vectors: float32 [256, 8, 512], P('hb', None, 'col'), may hold values from -6 to 6
- input_gate: float32 [256, 8], P('hb'), may hold values from -3 to 3
- forget_gate: float32 [256, 8], P('hb'), may hold values from -1 to 5
- output_gate_logits: float32 [256, 8, 512], P('hb', None, 'col'), may hold values from -6 to 6
- norm_gain: float32 [8, 512], P(None, 'col'), may hold values from 0.5 to 1.5
- out_weight: bfloat16 [8, 512, 4096], P('hb', 'col', 'row'), may hold values from -0.09375 to 0.09375
Outputs:
- layer_out: float32 [256, 4096], P('hb', 'row')
- readout: float32 [256, 8, 512], P('hb', None, 'col')
- refreshed_cell: float32 [256, 8, 256, 512], P('hb', None, 'row', 'col')
- new_normal: float32 [256, 8, 256], P('hb', None, 'row')
- new_stab: float32 [256, 8, 16], P('hb', None, 'row')
All inputs are finite; a program needn't handle non-finite values.
Results may differ from a plain program's by a relative error of at most 0.0029.
Values may be sent and summed in bfloat16 or wider, within the bound.
No kernel may reach another device: no remote copies, remote signals or barrier semaphores. Data moves between devices by JAX's collectives and lax.ppermute only.
A program may use at most 64 MiB of HBM per device.

v0:
```python
import jax
import jax.numpy as jnp
from jax import lax
from jax.sharding import Mesh
from jax.sharding import PartitionSpec as P

DK = 256
DV = 512
RBLK = 16
ROW = ("row_0", "row_1")


def all_in_one(x, axis):
    leaves = jax.tree.leaves(x)
    order = sorted(range(len(leaves)), key=lambda k: -leaves[k].size)
    width = (1, *leaves[order[0]].shape)[-1]
    lines = [
        jnp.pad(leaves[k].reshape(-1), (0, -leaves[k].size % width)).reshape(-1, width)
        for k in order
    ]
    both, at, found = (lax.all_gather(jnp.concatenate(lines), axis), 0, {})
    for k, line in zip(order, lines):
        share = both[:, at : at + len(line)].reshape(len(both), -1)
        found[k] = share[:, : leaves[k].size].reshape(-1, *leaves[k].shape)
        at += len(line)
    numbers = iter(range(len(leaves)))
    return jax.tree.map(lambda _: found[next(numbers)], x)


def combined_by_axis(x, axes, combine):
    for axis in axes:
        pieces = all_in_one(x, axis)
        x = jax.tree.map(lambda part: part[0], pieces)
        for k in range(1, lax.axis_size(axis)):
            x = combine(x, jax.tree.map(lambda part: part[k], pieces))
    return x


def sent_to_all(x, axis):
    copies = jnp.broadcast_to(x, (lax.axis_size(axis), *x.shape))
    return lax.all_to_all(copies, axis, split_axis=0, concat_axis=0, tiled=True)


def over_copies(x, axis):
    everything = sent_to_all(x, axis)
    return jnp.sum(everything, axis=0)


def together(arrays, axis):
    ends = [0]
    for a in arrays:
        ends.append(ends[-1] + a.size)
    running = over_copies(jnp.concatenate([a.ravel() for a in arrays]), axis)
    return tuple((running[b:e].reshape(a.shape) for a, b, e in zip(arrays, ends, ends[1:])))


def combine_pairs(left_pair, right_pair):
    joined = jnp.maximum(left_pair[0], right_pair[0])
    left_scale = jnp.exp(left_pair[0] - joined)
    right_scale = jnp.exp(right_pair[0] - joined)
    numerator = left_pair[1] * left_scale[:, :, None] + right_pair[1] * right_scale[:, :, None]
    denom = left_pair[2] * left_scale + right_pair[2] * right_scale
    return (joined, numerator, denom)


def local(
    cell_state,
    normalizer,
    stabilizer,
    queries,
    key_vectors,
    token_value_vectors,
    input_gate,
    forget_gate,
    output_gate_logits,
    norm_gain,
    out_weight,
):
    carried = jax.nn.log_sigmoid(forget_gate)[:, :, None] + stabilizer
    fresh = jnp.maximum(carried, input_gate[:, :, None])
    keep = jnp.repeat(jnp.exp(carried - fresh), RBLK, axis=2)
    admit = jnp.repeat(jnp.exp(input_gate[:, :, None] - fresh), RBLK, axis=2)
    scaled = key_vectors * DK ** (-0.5)
    refreshed_cell = (
        keep[:, :, :, None] * cell_state
        + (admit * scaled)[:, :, :, None] * token_value_vectors[:, :, None, :]
    )
    new_normal = keep * normalizer + admit * scaled
    local_top = jnp.max(fresh, axis=2)
    weight_matrix = jnp.repeat(jnp.exp(fresh - local_top[:, :, None]), RBLK, axis=2) * queries
    numerator = jnp.einsum(
        "bhkv,bhk->bhv", refreshed_cell, weight_matrix, precision=lax.Precision.HIGHEST
    )
    denom = jnp.sum(new_normal * weight_matrix, axis=2)
    top, numerator, denom = combined_by_axis((local_top, numerator, denom), ROW, combine_pairs)
    readout = numerator / jnp.maximum(jnp.abs(denom), jnp.exp(-top))[:, :, None]
    running_totals, squares = together(
        (jnp.sum(readout, axis=2), jnp.sum(readout * readout, axis=2)), "col"
    )
    mean = running_totals / DV
    var = squares / DV - mean * mean
    normed = (readout - mean[:, :, None]) * lax.rsqrt(var + 1e-06)[:, :, None]
    gated = (normed * norm_gain * jax.nn.sigmoid(output_gate_logits)).astype(jnp.bfloat16)
    seq_rows = gated.shape[0]
    out_cols = out_weight.shape[2]
    partial_value = jnp.dot(
        gated.reshape(seq_rows, -1),
        lax.all_gather(out_weight, "hb", axis=0, tiled=True).reshape(-1, out_cols),
        preferred_element_type=jnp.float32,
    )
    layer_out = over_copies(partial_value, "col")
    return (layer_out, readout, refreshed_cell, new_normal, fresh)


def solution(mesh):
    torus = Mesh(
        mesh.devices.reshape(mesh.shape["hb"], 8, 2, mesh.shape["col"]),
        ("hb", "row_0", "row_1", "col"),
    )
    in_specs = (
        P("hb", None, ROW, "col"),
        P("hb", None, ROW),
        P("hb", None, ROW),
        P("hb", None, ROW),
        P("hb", None, ROW),
        P("hb", None, "col"),
        P("hb", None),
        P("hb", None),
        P("hb", None, "col"),
        P(None, "col"),
        P("hb", "col", ROW),
    )
    out_specs = (
        P("hb", ROW),
        P("hb", None, "col"),
        P("hb", None, ROW, "col"),
        P("hb", None, ROW),
        P("hb", None, ROW),
    )
    return jax.shard_map(local, mesh=torus, in_specs=in_specs, out_specs=out_specs, check_vma=False)
```

profile of v0, /device:TPU:1, one launch (start us, length us, event | category | flops | bytes accessed | tf_op | source)
XLA Modules:
  0.0 107.4 jit_solution(9087296757668042198)
XLA Ops:
  7.2 0.7 fusion.24
  7.9 0.7 subtract_exponential_fusion.2
  8.6 0.1 copy.35
  8.7 0.7 exponential_multiply_fusion
  9.4 0.1 copy.33
  9.5 1.6 %multiply_reduce_fusion.1 = (f32[64,8]{0,1:T(8,128)S(1)}, f32[64,8,16]{0,2,1:T(8,128)}, f32[64,8,16]{0,2,1:T(8,128)S(1)}, f32[64,8,16,1]{0,2,1,3:T(8,128)S(1)}) fusion(f32[64,8,16]{0,2,1:T(8,128)} %param.14, f32[64,8]{0,1:T(8,128)S(1)} %bitcast.431, f32[64,8,16]{0,2,1:T(8,128)} %param.12, f32[64,8]{0,1:T(8,128)S(1)} %bitcast.426, f32[64,8,16]{0,2,1:T(8,128)} %param.15, ...), kind=kLoop, calls=%fused_computation.41 | loop fusion | flops 48640 | bytes 204800 | tf_op jit(solution)/shard_map/reduce_sum | solution.py:94
  11.1 0.1 copy.34
  11.2 0.1 copy.39
  11.4 0.1 copy.36
  11.5 0.1 reshape.563
  11.6 0.1 reshape.561
  11.6 4.0 %multiply_add_fusion = f32[64,8,16,128]{3,2,1,0:T(8,128)S(1)} fusion(f32[64,8,16,128]{3,2,1,0:T(8,128)} %param.11, f32[64,8,128]{2,1,0:T(8,128)} %param.16, f32[64,8,16]{2,1,0:T(8,128)S(1)} %copy.34, f32[64,8]{1,0:T(8,128)S(1)} %copy.33), kind=kLoop, calls=%fused_computation | loop fusion | flops 3145728 | bytes 8685568 | tf_op jit(solution)/shard_map/add | solution.py:85
  15.7 2.0 %copy-done = f32[64,8,16,128]{3,2,1,0:T(8,128)} copy-done((f32[64,8,16,128]{3,2,1,0:T(8,128)}, f32[64,8,16,128]{3,2,1,0:T(8,128)S(1)}, u32[]{:S(2)}) %copy-start) | copy-done | bytes 4194328
  17.7 4.0 %fusion.81 = f32[64,8,1,128]{3,2,1,0:T(1,128)S(1)} fusion(f32[64,8,16,128]{3,2,1,0:T(8,128)S(1)} %multiply_add_fusion, f32[64,8,16,1]{2,3,1,0:T(1,128)S(1)} %copy.39), kind=kOutput, calls=%fused_computation.160 | convolution fusion | flops 12582912 | bytes 4489216 | tf_op jit(solution)/shard_map/bhkv,bhk->bhv/dot_general | solution.py:91
  21.7 0.7 pad_maximum_fusion
  22.5 12.6 %all_gather.19 = bf16[8,128,256]{2,1,0:T(8,128)(2,1)S(1)} all-gather(bf16[2,128,256]{2,1,0:T(8,128)(2,1)S(1)} %copy-done.2), channel_id=1, replica_groups=mesh['hb'=4,'row_0'=8,'row_1'=2,'col'=4] {'hb'}, dimensions={0}, use_global_device_ids=true | all-gather | bytes 655360 | tf_op jit(solution)/shard_map/all_gather | solution.py:108
  35.1 27.9 %all-gather.4.cloned.1.call-done = f32[4160,128]{1,0:T(8,128)} async-done(((f32[520,128]{1,0:T(8,128)}), f32[4160,128]{1,0:T(8,128)}) %all-gather.4.cloned.1.call-update) | async-done | bytes 2129936 | tf_op jit(solution)/shard_map/all_gather | solution.py:21
  63.0 0.7 fusion.67
  63.7 0.8 fusion.28
  64.5 0.7 fusion.66
  65.2 0.7 fusion.64
  65.9 0.7 fusion.62
  66.6 2.5 %fusion.1 = f32[512,128]{1,0:T(8,128)S(1)} fusion(f32[8,520,128]{2,1,0:T(8,128)} %bitcast.423, f32[512]{0:T(512)S(1)} %get-tuple-element.37, f32[512]{0:T(512)S(1)} %get-tuple-element.34, f32[512]{0:T(512)S(1)} %get-tuple-element.36, f32[512]{0:T(512)S(1)} %get-tuple-element.35, f32[512]{0:T(512)S(1)} %get-tuple-element.33, f32[512]{0:T(512)S(1)} %get-tuple-element.31, ...), kind=kLoop, calls=%fused_computation.6 | loop fusion | flops 1376256 | bytes 2387968 | tf_op jit(solution)/shard_map/add | solution.py:61
  69.1 7.4 %all-gather.1 = f32[1040,128]{1,0:T(8,128)S(1)} all-gather(f32[520,128]{1,0:T(8,128)S(1)} %pad_maximum_fusion.1), channel_id=3, replica_groups=mesh['hb'=4,'row_0'=8,'row_1'=2,'col'=4] {'row_1'}, dimensions={0}, use_global_device_ids=true | all-gather | bytes 798720 | tf_op jit(solution)/shard_map/all_gather | solution.py:21
  76.6 0.4 fusion.78
  77.0 0.6 broadcast_in_dim.10
  77.6 9.4 %all-to-all-start = ((f32[4,1,1024]{2,1,0:T(1,128)}), f32[4,1,1024]{2,1,0:T(1,128)S(1)}, u32[]{:S(2)}, u32[]{:S(2)}) async-start(f32[4,1,1024]{2,1,0:T(1,128)} %broadcast_in_dim.10), calls=%async_computation | async-start | bytes 32768 | tf_op jit(solution)/shard_map/all_to_all | solution.py:41
  87.4 2.8 %all-to-all-done = f32[4,1,1024]{2,1,0:T(1,128)S(1)} async-done(((f32[4,1,1024]{2,1,0:T(1,128)}), f32[4,1,1024]{2,1,0:T(1,128)S(1)}, u32[]{:S(2)}, u32[]{:S(2)}) %all-to-all-start) | async-done | bytes 16416 | tf_op jit(solution)/shard_map/all_to_all | solution.py:41
  90.4 1.1 %multiply_convert_fusion = (bf16[64,8,128]{2,1,0:T(8,128)(2,1)S(1)}, f32[64,8,128]{2,1,0:T(8,128)}) fusion(f32[64,8,128]{2,1,0:T(8,128)S(1)} %copy-done.1, f32[8,128]{1,0:T(8,128)S(1)} %copy-done.4, f32[64,8]{1,0:T(8,128)S(1)} %get-tuple-element.53, f32[64,8]{1,0:T(8,128)S(1)} %div.32, f32[64,8]{1,0:T(8,128)S(1)} %get-tuple-element.47, ...), kind=kLoop, calls=%fused_computation.37 | loop fusion | flops 786432 | bytes 1193984 | tf_op jit(solution)/shard_map/convert_element_type | solution.py:103
  91.5 0.2 convolution_bitcast_fusion
  91.8 8.1 %all_to_all.11 = f32[4,64,256]{2,1,0:T(8,128)S(1)} all-to-all(f32[4,64,256]{2,1,0:T(8,128)S(1)} %broadcast_in_dim.11), channel_id=1, replica_groups=mesh['hb'=4,'row_0'=8,'row_1'=2,'col'=4] {'col'}, dimensions={0} | all-to-all | bytes 524288 | tf_op jit(solution)/shard_map/all_to_all | solution.py:41
  99.9 0.6 reduce_sum.49
  (25 shorter events, 0.7 us)
Async XLA Ops:
  7.2 55.8 %all-gather.4.cloned.1.call-start = ((), (), s32[]{:S(2)}) async-start(), calls=%async_computation.2 | async-start | bytes 2396160 | tf_op jit(solution)/shard_map/all_gather | solution.py:21
  8.6 7.0 %copy-start.3 = (f32[64,1,8]{0,2,1:T(8,128)}, f32[64,1,8]{0,2,1:T(8,128)S(1)}, u32[]{:S(2)}) copy-start(f32[64,1,8]{0,2,1:T(8,128)S(1)} %get-tuple-element.55) | copy-start | bytes 6148
  15.7 2.0 %copy-start = (f32[64,8,16,128]{3,2,1,0:T(8,128)}, f32[64,8,16,128]{3,2,1,0:T(8,128)S(1)}, u32[]{:S(2)}) copy-start(f32[64,8,16,128]{3,2,1,0:T(8,128)S(1)} %multiply_add_fusion) | copy-start | bytes 12582916
  17.7 4.8 %copy-start.2 = (bf16[2,128,256]{2,1,0:T(8,128)(2,1)S(1)}, bf16[2,128,256]{2,1,0:T(8,128)(2,1)}, u32[]{:S(2)}) copy-start(bf16[2,128,256]{2,1,0:T(8,128)(2,1)} %param.21) | copy-start | bytes 393220
  21.7 68.7 %copy-start.1 = (f32[64,8,128]{2,1,0:T(8,128)S(1)}, f32[64,8,128]{2,1,0:T(8,128)}, u32[]{:S(2)}) copy-start(f32[64,8,128]{2,1,0:T(8,128)} %param.19) | copy-start | bytes 786436
  21.7 68.7 %copy-start.4 = (f32[8,128]{1,0:T(8,128)S(1)}, f32[8,128]{1,0:T(8,128)}, u32[]{:S(2)}) copy-start(f32[8,128]{1,0:T(8,128)} %param.20) | copy-start | bytes 12292
  77.6 12.5 %all-to-all-start = ((f32[4,1,1024]{2,1,0:T(1,128)}), f32[4,1,1024]{2,1,0:T(1,128)S(1)}, u32[]{:S(2)}, u32[]{:S(2)}) async-start(f32[4,1,1024]{2,1,0:T(1,128)} %broadcast_in_dim.10), calls=%async_computation | async-start | bytes 32768 | tf_op jit(solution)/shard_map/all_to_all | solution.py:41
Sparse Core Ops, SparseCore 0:
  22.6 40.3 all-gather.3
where the time goes:
time: 108 us; the launch traced here: 107 us
  waiting for transfers between devices  30.7 us (28%)
  blocking collectives  28.1 us (26%)
  other arithmetic  16.8 us (16%)
  between operations  14.2 us (13%)
  starting transfers between devices  9.42 us (9%)
  matrix products  4.21 us (4%)
  local copies, waits for them, and re-layouts  3.9 us (4%)
    all_gather x1, waiting for transfers between devices, all_in_one(): both, at, found = (lax.all_gather(jnp.concatenate(lines), axis), 0, {})  27.9 us
    all_gather x1, blocking collectives, local(): lax.all_gather(out_weight, 'hb', axis=0, tiled=True).reshape(-1, out_cols)  12.6 us
    all_to_all x1, starting transfers between devices, sent_to_all(): return lax.all_to_all(copies, axis, split_axis=0, concat_axis=0, tiled=True)  9.38 us
    all_to_all x1, blocking collectives, sent_to_all(): return lax.all_to_all(copies, axis, split_axis=0, concat_axis=0, tiled=True)  8.09 us
    all_gather x1, blocking collectives, all_in_one(): both, at, found = (lax.all_gather(jnp.concatenate(lines), axis), 0, {})  7.44 us
    add x1, other arithmetic, local(): keep[:, :, :, None] * cell_state  4.01 us
    dot_general x1, matrix products, local(): jnp.einsum('bhkv,bhk->bhv', refreshed_cell, weight_matrix, precision=lax....  4.01 us
    all_to_all x1, waiting for transfers between devices, sent_to_all(): return lax.all_to_all(copies, axis, split_axis=0, concat_axis=0, tiled=True)  2.76 us
  transfers between devices with their start and end apart: 2, of which 2 were waited for; matrix products, arithmetic and copies ran while one was open for 0% of the time, Pallas kernels for 0%

commit v1 on v0

--- a/solution.py
+++ b/solution.py
@@ -8,6 +8,11 @@
 DV = 512
 RBLK = 16
 ROW = ("row_0", "row_1")
+
+
+def tiled_gather(x, axis, dim):
+    copies = jnp.concatenate([x] * lax.axis_size(axis), axis=dim)
+    return lax.all_to_all(copies, axis, dim, dim, tiled=True)
 
 
 def all_in_one(x, axis):
@@ -105,7 +110,7 @@
     out_cols = out_weight.shape[2]
     partial_value = jnp.dot(
         gated.reshape(seq_rows, -1),
-        lax.all_gather(out_weight, "hb", axis=0, tiled=True).reshape(-1, out_cols),
+        tiled_gather(out_weight, "hb", 0).reshape(-1, out_cols),
         preferred_element_type=jnp.float32,
     )
     layer_out = over_copies(partial_value, "col")

time: 108 us -> 120 us (1.11)
  waiting for transfers between devices: 30.7 us -> 49.3 us
  blocking collectives: 28.1 us -> 17 us
  starting transfers between devices: 9.42 us -> 13.4 us
    all_gather x1 -> x0, blocking collectives: 12.6 us -> none  [local(): lax.all_gather(out_weight, 'hb', axis=0, tiled=True).reshape(-1, out_cols)]
    all_gather x1, waiting for transfers between devices: 27.9 us -> 39.7 us  [all_in_one(): both, at, found = (lax.all_gather(jnp.concatenate(lines), axis), 0, {})]
    all_to_all x0 -> x1, waiting for transfers between devices: none -> 6.89 us  [tiled_gather(): return lax.all_to_all(copies, axis, dim, dim, tiled=True)]
    all_to_all x0 -> x1, starting transfers between devices: none -> 4 us  [tiled_gather(): return lax.all_to_all(copies, axis, dim, dim, tiled=True)]
    all_to_all x1, blocking collectives: 8.09 us -> 9.52 us  [sent_to_all(): return lax.all_to_all(copies, axis, split_axis=0, concat_axis=0, tiled=True)]
  transfers between devices with their start and end apart: 2 -> 3, of which waited for: 2 -> 3; matrix products, arithmetic and copies ran while one was open for 0% -> 2% of each run, Pallas kernels for 0% -> 0%
where the time goes in v1:
time: 120 us
  waiting for transfers between devices  49.3 us (41%)
  other arithmetic  17.6 us (15%)
  blocking collectives  17 us (14%)
  between operations  14.2 us (12%)
  starting transfers between devices  13.4 us (11%)
  matrix products  4.21 us (4%)
  local copies, waits for them, and re-layouts  3.9 us (3%)
    all_gather x1, waiting for transfers between devices, all_in_one(): both, at, found = (lax.all_gather(jnp.concatenate(lines), axis), 0, {})  39.7 us
    all_to_all x1, blocking collectives, sent_to_all(): return lax.all_to_all(copies, axis, split_axis=0, concat_axis=0, tiled=True)  9.52 us
    all_to_all x1, starting transfers between devices, sent_to_all(): return lax.all_to_all(copies, axis, split_axis=0, concat_axis=0, tiled=True)  9.38 us
    all_gather x1, blocking collectives, all_in_one(): both, at, found = (lax.all_gather(jnp.concatenate(lines), axis), 0, {})  7.44 us
    all_to_all x1, waiting for transfers between devices, tiled_gather(): return lax.all_to_all(copies, axis, dim, dim, tiled=True)  6.89 us
    add x1, other arithmetic, local(): keep[:, :, :, None] * cell_state  4.01 us
    dot_general x1, matrix products, local(): jnp.einsum('bhkv,bhk->bhv', refreshed_cell, weight_matrix, precision=lax....  4.01 us
    all_to_all x1, starting transfers between devices, tiled_gather(): return lax.all_to_all(copies, axis, dim, dim, tiled=True)  4 us
  transfers between devices with their start and end apart: 3, of which 3 were waited for; matrix products, arithmetic and copies ran while one was open for 2% of the time, Pallas kernels for 0%

profile of v1, /device:TPU:1, one launch (start us, length us, event | category | flops | bytes accessed | tf_op | source)
XLA Modules:
  0.0 119.7 jit_solution(4297350612831598413)
XLA Ops:
  7.2 0.7 fusion.24
  7.9 0.7 subtract_exponential_fusion.2
  8.7 0.7 exponential_multiply_fusion
  9.4 0.1 copy.33
  9.5 1.6 %multiply_reduce_fusion.1 = (f32[64,8]{0,1:T(8,128)S(1)}, f32[64,8,16]{0,2,1:T(8,128)}, f32[64,8,16]{0,2,1:T(8,128)S(1)}, f32[64,8,16,1]{0,2,1,3:T(8,128)S(1)}) fusion(f32[64,8,16]{0,2,1:T(8,128)} %param.14, f32[64,8]{0,1:T(8,128)S(1)} %bitcast.431, f32[64,8,16]{0,2,1:T(8,128)} %param.12, f32[64,8]{0,1:T(8,128)S(1)} %bitcast.426, f32[64,8,16]{0,2,1:T(8,128)} %param.15, ...), kind=kLoop, calls=%fused_computation.42 | loop fusion | flops 48640 | bytes 204800 | tf_op jit(solution)/shard_map/reduce_sum | solution.py:99
  11.1 0.1 copy.34
  11.2 0.1 copy.39
  11.5 0.1 reshape.563
  11.6 0.1 reshape.561
  11.6 4.0 %multiply_add_fusion = f32[64,8,16,128]{3,2,1,0:T(8,128)S(1)} fusion(f32[64,8,16,128]{3,2,1,0:T(8,128)} %param.11, f32[64,8,128]{2,1,0:T(8,128)} %param.16, f32[64,8,16]{2,1,0:T(8,128)S(1)} %copy.34, f32[64,8]{1,0:T(8,128)S(1)} %copy.33), kind=kLoop, calls=%fused_computation | loop fusion | flops 3145728 | bytes 8685568 | tf_op jit(solution)/shard_map/add | solution.py:90
  15.7 2.0 %copy-done = f32[64,8,16,128]{3,2,1,0:T(8,128)} copy-done((f32[64,8,16,128]{3,2,1,0:T(8,128)}, f32[64,8,16,128]{3,2,1,0:T(8,128)S(1)}, u32[]{:S(2)}) %copy-start) | copy-done | bytes 4194328
  17.7 4.0 %fusion.81 = f32[64,8,1,128]{3,2,1,0:T(1,128)S(1)} fusion(f32[64,8,16,128]{3,2,1,0:T(8,128)S(1)} %multiply_add_fusion, f32[64,8,16,1]{2,3,1,0:T(1,128)S(1)} %copy.39), kind=kOutput, calls=%fused_computation.161 | convolution fusion | flops 12582912 | bytes 4489216 | tf_op jit(solution)/shard_map/bhkv,bhk->bhv/dot_general | solution.py:96
  21.7 0.7 pad_maximum_fusion.1
  22.5 0.8 pad_maximum_fusion
  23.3 39.7 %all-gather.4.cloned.1.call-done = f32[4160,128]{1,0:T(8,128)} async-done(((f32[520,128]{1,0:T(8,128)}), f32[4160,128]{1,0:T(8,128)}) %all-gather.4.cloned.1.call-update) | async-done | bytes 2129936 | tf_op jit(solution)/shard_map/all_gather | solution.py:26
  63.0 0.7 fusion.67
  63.7 0.8 fusion.28
  64.5 0.7 fusion.66
  65.2 0.7 fusion.64
  65.9 0.7 fusion.62
  66.6 2.5 %fusion.1 = f32[512,128]{1,0:T(8,128)S(1)} fusion(f32[8,520,128]{2,1,0:T(8,128)} %bitcast.423, f32[512]{0:T(512)S(1)} %get-tuple-element.37, f32[512]{0:T(512)S(1)} %get-tuple-element.34, f32[512]{0:T(512)S(1)} %get-tuple-element.36, f32[512]{0:T(512)S(1)} %get-tuple-element.35, f32[512]{0:T(512)S(1)} %get-tuple-element.33, f32[512]{0:T(512)S(1)} %get-tuple-element.31, ...), kind=kLoop, calls=%fused_computation.7 | loop fusion | flops 1376256 | bytes 2387968 | tf_op jit(solution)/shard_map/add | solution.py:66
  69.1 7.4 %all-gather.1 = f32[1040,128]{1,0:T(8,128)S(1)} all-gather(f32[520,128]{1,0:T(8,128)S(1)} %pad_maximum_fusion.2), channel_id=3, replica_groups=mesh['hb'=4,'row_0'=8,'row_1'=2,'col'=4] {'row_1'}, dimensions={0}, use_global_device_ids=true | all-gather | bytes 798720 | tf_op jit(solution)/shard_map/all_gather | solution.py:26
  76.6 0.4 fusion.78
  77.0 0.6 broadcast_in_dim.10
  77.6 9.4 %all-to-all-start = ((f32[4,1,1024]{2,1,0:T(1,128)}), f32[4,1,1024]{2,1,0:T(1,128)S(1)}, u32[]{:S(2)}, u32[]{:S(2)}) async-start(f32[4,1,1024]{2,1,0:T(1,128)} %broadcast_in_dim.10), calls=%async_computation | async-start | bytes 32768 | tf_op jit(solution)/shard_map/all_to_all | solution.py:46
  87.4 2.8 %all-to-all-done = f32[4,1,1024]{2,1,0:T(1,128)S(1)} async-done(((f32[4,1,1024]{2,1,0:T(1,128)}), f32[4,1,1024]{2,1,0:T(1,128)S(1)}, u32[]{:S(2)}, u32[]{:S(2)}) %all-to-all-start) | async-done | bytes 16416 | tf_op jit(solution)/shard_map/all_to_all | solution.py:46
  90.2 4.0 %all-to-all-start.1 = ((bf16[8,128,256]{2,1,0:T(8,128)(2,1)}), bf16[8,128,256]{2,1,0:T(8,128)(2,1)S(1)}, u32[]{:S(2)}, u32[]{:S(2)}) async-start(bf16[8,128,256]{2,1,0:T(8,128)(2,1)} %pad_maximum_fusion), calls=%async_computation.1 | async-start | bytes 1048576 | tf_op jit(solution)/shard_map/all_to_all | solution.py:15
  94.4 1.1 multiply_convert_fusion
  95.5 6.9 %all-to-all-done.1 = bf16[8,128,256]{2,1,0:T(8,128)(2,1)S(1)} async-done(((bf16[8,128,256]{2,1,0:T(8,128)(2,1)}), bf16[8,128,256]{2,1,0:T(8,128)(2,1)S(1)}, u32[]{:S(2)}, u32[]{:S(2)}) %all-to-all-start.1) | async-done | bytes 524320 | tf_op jit(solution)/shard_map/all_to_all | solution.py:15
  102.4 0.2 convolution_bitcast_fusion
  102.7 9.5 %all_to_all.16 = f32[4,64,256]{2,1,0:T(8,128)S(1)} all-to-all(f32[4,64,256]{2,1,0:T(8,128)S(1)} %broadcast_in_dim.11), channel_id=1, replica_groups=mesh['hb'=4,'row_0'=8,'row_1'=2,'col'=4] {'col'}, dimensions={0} | all-to-all | bytes 524288 | tf_op jit(solution)/shard_map/all_to_all | solution.py:46
  112.2 0.6 reduce_sum.49
  (27 shorter events, 0.9 us)
Async XLA Ops:
  7.2 55.8 %all-gather.4.cloned.1.call-start = ((), (), s32[]{:S(2)}) async-start(), calls=%async_computation.3 | async-start | bytes 2396160 | tf_op jit(solution)/shard_map/all_gather | solution.py:26
  8.6 7.0 %copy-start.3 = (f32[64,1,8]{0,2,1:T(8,128)}, f32[64,1,8]{0,2,1:T(8,128)S(1)}, u32[]{:S(2)}) copy-start(f32[64,1,8]{0,2,1:T(8,128)S(1)} %get-tuple-element.55) | copy-start | bytes 6148
  15.7 2.0 %copy-start = (f32[64,8,16,128]{3,2,1,0:T(8,128)}, f32[64,8,16,128]{3,2,1,0:T(8,128)S(1)}, u32[]{:S(2)}) copy-start(f32[64,8,16,128]{3,2,1,0:T(8,128)S(1)} %multiply_add_fusion) | copy-start | bytes 12582916
  17.7 4.8 %copy-start.2 = (bf16[2,128,256]{2,1,0:T(8,128)(2,1)S(1)}, bf16[2,128,256]{2,1,0:T(8,128)(2,1)}, u32[]{:S(2)}) copy-start(bf16[2,128,256]{2,1,0:T(8,128)(2,1)} %param.21) | copy-start | bytes 393220
  21.7 72.7 %copy-start.1 = (f32[64,8,128]{2,1,0:T(8,128)S(1)}, f32[64,8,128]{2,1,0:T(8,128)}, u32[]{:S(2)}) copy-start(f32[64,8,128]{2,1,0:T(8,128)} %param.19) | copy-start | bytes 786436
  21.7 72.7 %copy-start.4 = (f32[8,128]{1,0:T(8,128)S(1)}, f32[8,128]{1,0:T(8,128)}, u32[]{:S(2)}) copy-start(f32[8,128]{1,0:T(8,128)} %param.20) | copy-start | bytes 12292
  77.6 12.5 %all-to-all-start = ((f32[4,1,1024]{2,1,0:T(1,128)}), f32[4,1,1024]{2,1,0:T(1,128)S(1)}, u32[]{:S(2)}, u32[]{:S(2)}) async-start(f32[4,1,1024]{2,1,0:T(1,128)} %broadcast_in_dim.10), calls=%async_computation | async-start | bytes 32768 | tf_op jit(solution)/shard_map/all_to_all | solution.py:46
  90.2 12.3 %all-to-all-start.1 = ((bf16[8,128,256]{2,1,0:T(8,128)(2,1)}), bf16[8,128,256]{2,1,0:T(8,128)(2,1)S(1)}, u32[]{:S(2)}, u32[]{:S(2)}) async-start(bf16[8,128,256]{2,1,0:T(8,128)(2,1)} %pad_maximum_fusion), calls=%async_computation.1 | async-start | bytes 1048576 | tf_op jit(solution)/shard_map/all_to_all | solution.py:15
Sparse Core Ops, SparseCore 0:
  22.6 40.3 all-gather.3
